TPU v7x, 256 devices: a whole 4x4x8 slice. The times are simulated.
256 devices in a mesh: dp: 16 (over z, core), mp: 16 (over y, x).
Axes of the slice: x: 4, y: 4, z: 8, core: 2. Of those that a mesh axis runs over, the one named last changes fastest.
Arguments:
- candidates: bfloat16 [4096, 4096], P('dp', 'mp'), may hold values from -6 to 6
- hold_gate: bfloat16 [4096, 8192], P(None, 'mp'), may hold values from -0.09375 to 0.09375
- hold_up: bfloat16 [4096, 8192], P(None, 'mp'), may hold values from -0.09375 to 0.09375
- probe: float32 [8192], P('mp'), as said below
- chosen: int32 [16, 192], replicated, may hold values from 0 to 4095, as said below
- counts: int32 [16], replicated, may hold values from 24 to 192, as said below
- gate_w: bfloat16 [4096, 14336], P('dp', 'mp'), may hold values from -0.09375 to 0.09375
- up_w: bfloat16 [4096, 14336], P('dp', 'mp'), may hold values from -0.09375 to 0.09375
- cotangent: bfloat16 [3072, 14336], P('dp', 'mp'), may hold values from -6 to 6
Outputs:
- grad_gate: bfloat16 [4096, 14336], P('dp', 'mp')
- grad_up: bfloat16 [4096, 14336], P('dp', 'mp')
- hidden: bfloat16 [3072, 14336], P('dp', 'mp')
- cand_weight: float32 [4096], P('dp')
Inputs may be any that keep to these rules, and one draw needn't show every extreme that they name: `chosen`: all entries are distinct candidate indices. `counts`: exactly one training shard uses all 192 slots in every draw. `probe`: magnitudes at most 12 / sqrt(8192).
All inputs are finite; a program needn't handle non-finite values.
Results may differ from a plain program's by a relative error of at most 0.0057.
Values may be sent and summed in bfloat16 or wider, within the bound.
A program may use at most 128 MiB of HBM per device.

v0:
```python
import jax
import jax.numpy as jnp
from jax import lax
from jax.sharding import PartitionSpec as P


def gather_by_a2a(x, axis_name, axis):
    parts = lax.psum(1, axis_name)
    stacked = lax.all_to_all(
        jnp.broadcast_to(x[None], (parts,) + x.shape),
        axis_name,
        split_axis=0,
        concat_axis=0,
        tiled=True,
    )
    stacked = jnp.moveaxis(stacked, 0, axis)
    shape = list(x.shape)
    shape[axis] *= parts
    return stacked.reshape(shape)


def on_device(candidates, hold_gate, hold_up, probe, chosen, counts, gate_w, up_w, cotangent):
    cand_dev = candidates.shape[0]
    shards = chosen.shape[0]
    slots = chosen.shape[1]
    width = candidates.shape[1]
    ff = gate_w.shape[1]
    merged = lax.all_gather(jnp.concatenate([candidates, gate_w], axis=1), "dp", axis=0, tiled=True)
    all_cands = merged[:, :width]
    full_w = (merged[:, width:], lax.all_gather(up_w, "dp", axis=0, tiled=True))
    own_index = lax.axis_index("dp")
    source = chosen // cand_dev
    local_row = (chosen % cand_dev).reshape(-1)
    valid = jnp.arange(slots, dtype=jnp.int32)[None, :] < counts[:, None]
    usable = (valid & (source == own_index)).reshape(-1)
    onehot = (
        (local_row[:, None] == jnp.arange(cand_dev, dtype=jnp.int32)[None, :]) & usable[:, None]
    ).astype(jnp.bfloat16)
    own_chosen = lax.dynamic_index_in_dim(chosen, own_index, 0, keepdims=False)
    own_valid = lax.dynamic_index_in_dim(valid, own_index, 0, keepdims=False)
    own_onehot = (
        (own_chosen[:, None] == jnp.arange(all_cands.shape[0], dtype=jnp.int32)[None, :])
        & own_valid[:, None]
    ).astype(jnp.bfloat16)
    row_slab = jnp.dot(own_onehot, all_cands, preferred_element_type=jnp.float32).astype(
        jnp.bfloat16
    )
    row_x = gather_by_a2a(row_slab, "mp", 1)
    parts = lax.psum(1, "dp")
    row_blocks = row_x.reshape(row_x.shape[0], parts, -1).transpose(1, 0, 2)
    row_slices = lax.all_to_all(row_blocks, "dp", split_axis=0, concat_axis=0, tiled=True)
    row_slices = row_slices.reshape(-1, row_blocks.shape[2])
    incoming = gather_by_a2a(candidates, "mp", 1)
    hold_g = jnp.dot(incoming, hold_gate, preferred_element_type=jnp.float32)
    hold_u = jnp.dot(incoming, hold_up, preferred_element_type=jnp.float32)
    partial_score = jnp.sum(jax.nn.silu(hold_g) * hold_u * probe[None, :], axis=1)
    score = jnp.sum(gather_by_a2a(partial_score[None, :], "mp", 0), axis=0)
    cand_weight = jax.nn.sigmoid(score)
    picked_weight = (
        jnp.dot(
            onehot, cand_weight.astype(jnp.bfloat16)[:, None], preferred_element_type=jnp.float32
        )
        .astype(jnp.bfloat16)
        .reshape(shards, slots)
    )
    arrived_weight = lax.all_to_all(picked_weight, "dp", split_axis=0, concat_axis=0, tiled=True)
    row_weight = jnp.sum(arrived_weight.astype(jnp.float32), axis=0)
    gate = jnp.dot(row_x, full_w[0], preferred_element_type=jnp.float32)
    up = jnp.dot(row_x, full_w[1], preferred_element_type=jnp.float32)
    hidden = (jax.nn.silu(gate) * up).astype(jnp.bfloat16)
    back = cotangent.astype(jnp.float32) * row_weight[:, None]
    sig = jax.nn.sigmoid(gate)
    d_up = (back * gate * sig).astype(jnp.bfloat16)
    d_gate = (back * up * sig * (1.0 + gate * (1.0 - sig))).astype(jnp.bfloat16)
    contract_rows = (((0,), (0,)), ((), ()))
    d_both, row_slices = lax.optimization_barrier(
        (jnp.concatenate([d_gate, d_up], axis=1), row_slices)
    )
    both_d = lax.all_gather(d_both, "dp", axis=0, tiled=True)
    grads = lax.dot_general(
        row_slices, both_d, contract_rows, preferred_element_type=jnp.float32
    ).astype(jnp.bfloat16)
    return (grads[:, :ff], grads[:, ff:], hidden, cand_weight)


def solution(mesh):
    placed = (
        P("dp", "mp"),
        P(None, "mp"),
        P(None, "mp"),
        P("mp"),
        P(),
        P(),
        P("dp", "mp"),
        P("dp", "mp"),
        P("dp", "mp"),
    )
    return jax.shard_map(
        on_device,
        mesh=mesh,
        in_specs=placed,
        out_specs=(P("dp", "mp"), P("dp", "mp"), P("dp", "mp"), P("dp")),
        check_vma=False,
    )
```

profile of v0, /device:TPU:1, one launch (start us, length us, event | category | flops | bytes accessed | tf_op | source)
XLA Modules:
  0.0 239.8 jit_solution(12118811220462123746)
XLA Ops:
  7.2 0.0 copy-start
  7.2 0.0 all-gather.4.cloned.1.call-start
  7.2 1.9 pad_maximum_fusion.1
  9.2 0.0 all-gather.4.cloned.1.call-update
  9.2 0.0 all-gather.6.cloned.1.call-start
  9.2 0.7 all-gather.6.cloned.1.call-update
  9.9 0.0 copy-done
  10.0 0.1 copy.22
  10.1 1.5 broadcast_in_dim.6
  11.6 0.0 copy-start.1
  11.6 0.0 copy-start.2
  11.6 7.7 %all-to-all-start = ((bf16[16,256,256]{1,2,0:T(8,128)(2,1)}), bf16[16,256,256]{1,2,0:T(8,128)(2,1)S(1)}, u32[]{:S(2)}, u32[]{:S(2)}) async-start(bf16[16,256,256]{1,2,0:T(8,128)(2,1)} %broadcast_in_dim.6), calls=%async_computation | async-start | bytes 4194304 | tf_op jit(solution)/shard_map/all_to_all | solution.py:9
  19.3 0.0 copy-done.1
  19.3 0.0 copy-done.2
  19.3 0.1 fusion.22
  19.4 30.8 %all-to-all-done = bf16[16,256,256]{1,2,0:T(8,128)(2,1)S(1)} async-done(((bf16[16,256,256]{1,2,0:T(8,128)(2,1)}), bf16[16,256,256]{1,2,0:T(8,128)(2,1)S(1)}, u32[]{:S(2)}, u32[]{:S(2)}) %all-to-all-start) | async-done | bytes 2097184 | tf_op jit(solution)/shard_map/all_to_all | solution.py:9
  50.3 0.0 copy-start.3
  50.3 0.0 copy-start.5
  50.3 3.7 %fusion.26 = f32[256,512]{1,0:T(8,128)S(1)} fusion(bf16[256,4096]{0,1:T(8,128)(2,1)S(1)} %bitcast.20, bf16[4096,512]{1,0:T(8,128)(2,1)} %param.10), kind=kOutput, calls=%fused_computation.42 | convolution fusion | flops 1073741824 | bytes 6815744 | tf_op jit(solution)/shard_map/dot_general | solution.py:54
  54.0 0.0 copy-done.3
  54.0 0.0 copy-done.5
  54.0 1.4 fusion.14
  55.4 0.6 broadcast_in_dim.7
  56.0 3.9 %all-to-all-start.1 = ((f32[16,1,256]{2,1,0:T(1,128)}), f32[16,1,256]{2,1,0:T(1,128)S(1)}, u32[]{:S(2)}, u32[]{:S(2)}) async-start(f32[16,1,256]{2,1,0:T(1,128)} %broadcast_in_dim.7), calls=%async_computation.1 | async-start | bytes 32768 | tf_op jit(solution)/shard_map/all_to_all | solution.py:9
  59.9 0.1 and.37
  60.0 0.1 eq.38
  60.1 6.2 %all-to-all-done.1 = f32[16,1,256]{2,1,0:T(1,128)S(1)} async-done(((f32[16,1,256]{2,1,0:T(1,128)}), f32[16,1,256]{2,1,0:T(1,128)S(1)}, u32[]{:S(2)}, u32[]{:S(2)}) %all-to-all-start.1) | async-done | bytes 16416 | tf_op jit(solution)/shard_map/all_to_all | solution.py:9
  66.3 0.6 fusion.24
  66.9 2.5 %fusion.6 = f32[1,3072]{1,0:T(1,128)S(1)} fusion(bf16[256,1]{0,1:T(2,128)(2,1)S(1)} %reshape.45, s32[3072]{0:T(1024)S(1)} %eq.38, pred[3072]{0:T(1024)(128)(4,1)S(1)} %and.37), kind=kOutput, calls=%fused_computation.7 | convolution fusion | flops 3145728 | bytes 28160 | tf_op jit(solution)/shard_map/dot_general | solution.py:60
  69.4 0.7 all_to_all.24
  70.1 11.0 %all-to-all-start.2 = ((bf16[16,1,192]{2,1,0:T(2,128)(2,1)}), bf16[16,1,192]{2,1,0:T(2,128)(2,1)S(1)}, u32[]{:S(2)}, u32[]{:S(2)}) async-start(bf16[16,1,192]{2,1,0:T(2,128)(2,1)} %all_to_all.24), calls=%async_computation.2 | async-start | bytes 32768 | tf_op jit(solution)/shard_map/all_to_all | solution.py:66
  81.1 0.0 all-gather.4.cloned.1.call-done
  81.2 2.4 fusion.15
  83.5 4.9 %all-to-all-done.2 = bf16[16,1,192]{2,1,0:T(2,128)(2,1)S(1)} async-done(((bf16[16,1,192]{2,1,0:T(2,128)(2,1)}), bf16[16,1,192]{2,1,0:T(2,128)(2,1)S(1)}, u32[]{:S(2)}, u32[]{:S(2)}) %all-to-all-start.2) | async-done | bytes 6176 | tf_op jit(solution)/shard_map/all_to_all | solution.py:66
  88.5 0.1 broadcast_in_dim.8
  88.6 25.6 %all_to_all.30 = bf16[16,192,256]{2,1,0:T(8,128)(2,1)} all-to-all(bf16[16,192,256]{2,1,0:T(8,128)(2,1)S(1)} %broadcast_in_dim.8), channel_id=1, replica_groups=mesh['dp'=16,'mp'=16] {'mp'}, dimensions={0} | all-to-all | bytes 3145728 | tf_op jit(solution)/shard_map/all_to_all | solution.py:9
  114.2 5.0 %all-to-all-start.4 = ((bf16[16,192,256]{2,1,0:T(8,128)(2,1)}), bf16[16,192,256]{2,1,0:T(8,128)(2,1)S(1)}, u32[]{:S(2)}, u32[]{:S(2)}) async-start(bf16[16,192,256]{2,1,0:T(8,128)(2,1)} %all_to_all.30), calls=%async_computation.4 | async-start | bytes 3145728 | tf_op jit(solution)/shard_map/all_to_all | solution.py:51
  119.3 0.0 all-gather.8.cloned.1.call-start
  119.3 1.6 copy.27
  121.0 0.0 copy-start.4
  121.0 5.9 %fusion = f32[192,896]{1,0:T(8,128)} fusion(bf16[192,4096]{1,0:T(8,128)(2,1)S(1)} %bitcast.22, bf16[4096,1152]{1,0:T(8,128)(2,1)} %all-gather.4.cloned.1.call-done), kind=kOutput, calls=%fused_computation | convolution fusion | flops 1409286144 | bytes 9601024 | tf_op jit(solution)/shard_map/dot_general | solution.py:68
  126.9 1.1 all-gather.6.cloned.1.call-done
  128.0 0.0 copy-done.4
  128.0 5.9 %multiply_convert_fusion = (bf16[192,896]{1,0:T(8,128)(2,1)}, bf16[192,896]{1,0:T(8,128)(2,1)S(1)}, bf16[192,896]{1,0:T(8,128)(2,1)S(1)}) fusion(f32[192,896]{1,0:T(8,128)} %fusion, f32[192]{0:T(256)S(1)} %convert_reduce_fusion, bf16[192,896]{1,0:T(8,128)(2,1)S(1)} %copy-done.4, bf16[192,4096]{1,0:T(8,128)(2,1)S(1)} %bitcast.23, ...), kind=kOutput, calls=%fused_computation.19 | convolution fusion | flops 1412382720 | bytes 10978048 | tf_op jit(solution)/shard_map/dot_general | solution.py:69
  133.9 0.9 pad_maximum_fusion
  134.8 23.4 %all-to-all-done.4 = bf16[16,192,256]{2,1,0:T(8,128)(2,1)S(1)} async-done(((bf16[16,192,256]{2,1,0:T(8,128)(2,1)}), bf16[16,192,256]{2,1,0:T(8,128)(2,1)S(1)}, u32[]{:S(2)}, u32[]{:S(2)}) %all-to-all-start.4) | async-done | bytes 1572896 | tf_op jit(solution)/shard_map/all_to_all | solution.py:51
  158.2 0.0 all-gather.8.cloned.1.call-update
  158.3 66.9 %all-gather.8.cloned.1.call-done = bf16[3072,1792]{1,0:T(8,128)(2,1)} async-done(((bf16[192,1792]{1,0:T(8,128)(2,1)}), bf16[3072,1792]{1,0:T(8,128)(2,1)}) %all-gather.8.cloned.1.call-update) | async-done | bytes 11010064 | tf_op jit(solution)/shard_map/all_gather | solution.py:79
  225.1 7.2 %convolution_convert_fusion = bf16[256,1792]{1,0:T(8,128)(2,1)S(1)} fusion(bf16[3072,256]{1,0:T(8,128)(2,1)S(1)} %bitcast.19, bf16[3072,1792]{1,0:T(8,128)(2,1)} %all-gather.8.cloned.1.call-done), kind=kOutput, calls=%fused_computation.8 | convolution fusion | flops 2819031040 | bytes 13500416 | tf_op jit(solution)/shard_map/dot_general | solution.py:80
  232.3 1.0 fusion.25
  (7 shorter events, 0.1 us)
Async XLA Ops:
  7.2 2.8 %copy-start = (bf16[256,256]{1,0:T(8,128)(2,1)S(1)}, bf16[256,256]{1,0:T(8,128)(2,1)}, u32[]{:S(2)}) copy-start(bf16[256,256]{1,0:T(8,128)(2,1)} %param.9) | copy-start | bytes 393220
  7.2 74.0 %all-gather.4.cloned.1.call-start = ((), (), s32[]{:S(2)}) async-start(), calls=%async_computation.5 | async-start | bytes 10027008 | tf_op jit(solution)/shard_map/all_gather | solution.py:28
  9.2 118.8 %all-gather.6.cloned.1.call-start = ((), (), s32[]{:S(2)}) async-start(), calls=%async_computation.6 | async-start | bytes 7798784 | tf_op jit(solution)/shard_map/all_gather | solution.py:30
  11.6 7.7 %copy-start.1 = (s32[16,192]{1,0:T(8,128)S(1)}, s32[16,192]{1,0:T(8,128)}, u32[]{:S(2)}) copy-start(s32[16,192]{1,0:T(8,128)} %param.13) | copy-start | bytes 36868
  11.6 7.7 %copy-start.2 = (s32[16]{0:T(128)S(1)}, s32[16]{0:T(128)}, u32[]{:S(2)}) copy-start(s32[16]{0:T(128)} %param.14) | copy-start | bytes 196
  11.6 38.7 %all-to-all-start = ((bf16[16,256,256]{1,2,0:T(8,128)(2,1)}), bf16[16,256,256]{1,2,0:T(8,128)(2,1)S(1)}, u32[]{:S(2)}, u32[]{:S(2)}) async-start(bf16[16,256,256]{1,2,0:T(8,128)(2,1)} %broadcast_in_dim.6), calls=%async_computation | async-start | bytes 4194304 | tf_op jit(solution)/shard_map/all_to_all | solution.py:9
  50.3 3.7 %copy-start.3 = (bf16[4096,512]{1,0:T(8,128)(2,1)S(1)}, bf16[4096,512]{1,0:T(8,128)(2,1)}, u32[]{:S(2)}) copy-start(bf16[4096,512]{1,0:T(8,128)(2,1)} %param.11) | copy-start | bytes 12582916
  50.3 3.7 %copy-start.5 = (f32[512]{0:T(512)S(1)}, f32[512]{0:T(512)}, u32[]{:S(2)}) copy-start(f32[512]{0:T(512)} %param.12) | copy-start | bytes 6148
  56.0 10.3 %all-to-all-start.1 = ((f32[16,1,256]{2,1,0:T(1,128)}), f32[16,1,256]{2,1,0:T(1,128)S(1)}, u32[]{:S(2)}, u32[]{:S(2)}) async-start(f32[16,1,256]{2,1,0:T(1,128)} %broadcast_in_dim.7), calls=%async_computation.1 | async-start | bytes 32768 | tf_op jit(solution)/shard_map/all_to_all | solution.py:9
  70.1 18.3 %all-to-all-start.2 = ((bf16[16,1,192]{2,1,0:T(2,128)(2,1)}), bf16[16,1,192]{2,1,0:T(2,128)(2,1)S(1)}, u32[]{:S(2)}, u32[]{:S(2)}) async-start(bf16[16,1,192]{2,1,0:T(2,128)(2,1)} %all_to_all.24), calls=%async_computation.2 | async-start | bytes 32768 | tf_op jit(solution)/shard_map/all_to_all | solution.py:66
  114.2 44.0 %all-to-all-start.4 = ((bf16[16,192,256]{2,1,0:T(8,128)(2,1)}), bf16[16,192,256]{2,1,0:T(8,128)(2,1)S(1)}, u32[]{:S(2)}, u32[]{:S(2)}) async-start(bf16[16,192,256]{2,1,0:T(8,128)(2,1)} %all_to_all.30), calls=%async_computation.4 | async-start | bytes 3145728 | tf_op jit(solution)/shard_map/all_to_all | solution.py:51
  119.3 105.9 %all-gather.8.cloned.1.call-start = ((), (), s32[]{:S(2)}) async-start(), calls=%async_computation.7 | async-start | bytes 11698176 | tf_op jit(solution)/shard_map/all_gather | solution.py:79
  121.0 7.0 %copy-start.4 = (bf16[192,896]{1,0:T(8,128)(2,1)S(1)}, bf16[192,896]{1,0:T(8,128)(2,1)}, u32[]{:S(2)}) copy-start(bf16[192,896]{1,0:T(8,128)(2,1)} %param.17) | copy-start | bytes 1032196
Sparse Core Ops, SparseCore 0:
  9.8 64.9 all-gather.3
  76.7 51.3 all-gather.5
  158.4 66.7 all-gather.7
where the time goes:
time: 240 us
  waiting for transfers between devices  134 us (56%)
  matrix products  28.9 us (12%)
  starting transfers between devices  27.7 us (12%)
  blocking collectives  25.6 us (11%)
  between operations  13.9 us (6%)
  local copies, waits for them, and re-layouts  5.97 us (2%)
  other arithmetic  3.59 us (1%)
    all_gather x1, waiting for transfers between devices, on_device(): both_d = lax.all_gather(d_both, 'dp', axis=0, tiled=True)  66.9 us
    all_to_all x2, waiting for transfers between devices, gather_by_a2a(): lax.all_to_all(jnp.broadcast_to(x[None], (parts,) + x.shape), axis_name,...  37.1 us
    all_to_all x1, blocking collectives, gather_by_a2a(): lax.all_to_all(jnp.broadcast_to(x[None], (parts,) + x.shape), axis_name,...  25.6 us
    all_to_all x1, waiting for transfers between devices, on_device(): lax.all_to_all(row_blocks, 'dp', split_axis=0, concat_axis=0, tiled=True)  23.4 us
    all_to_all x2, starting transfers between devices, gather_by_a2a(): lax.all_to_all(jnp.broadcast_to(x[None], (parts,) + x.shape), axis_name,...  11.6 us
    all_to_all x1, starting transfers between devices, on_device(): lax.all_to_all(picked_weight, 'dp', split_axis=0, concat_axis=0, tiled=True)  11 us
    dot_general x1, matrix products, on_device(): lax.dot_general(row_slices, both_d, contract_rows, preferred_element_type...  7.17 us
    dot_general x1, matrix products, on_device(): up = jnp.dot(row_x, full_w[1], preferred_element_type=jnp.float32)  5.92 us
  transfers between devices with their start and end apart: 7, of which 6 were waited for; matrix products, arithmetic and copies ran while one was open for 12% of the time, Pallas kernels for 0%

commit v1 on v0

--- a/solution.py
+++ b/solution.py
@@ -76,7 +76,26 @@
     d_both, row_slices = lax.optimization_barrier(
         (jnp.concatenate([d_gate, d_up], axis=1), row_slices)
     )
-    both_d = lax.all_gather(d_both, "dp", axis=0, tiled=True)
+    kept_arr, e_now, v1 = (lax.psum(1, "dp"), lax.axis_index("dp"), d_both.shape[0])
+    fields = [j * kept_arr if dev_i == 0 else j for dev_i, j in enumerate(d_both.shape)]
+    both_d = lax.dynamic_update_slice_in_dim(
+        jnp.zeros(fields, d_both.dtype), d_both, e_now * v1, axis=0
+    )
+    current_value = local_next = d_both
+    for at in range(1, kept_arr // 2 + 1):
+        current_value = lax.ppermute(
+            current_value, "dp", [(dev_i, (dev_i + 1) % kept_arr) for dev_i in range(kept_arr)]
+        )
+        both_d = lax.dynamic_update_slice_in_dim(
+            both_d, current_value, (e_now - at) % kept_arr * v1, axis=0
+        )
+        if 2 * at < kept_arr:
+            local_next = lax.ppermute(
+                local_next, "dp", [(dev_i, (dev_i - 1) % kept_arr) for dev_i in range(kept_arr)]
+            )
+            both_d = lax.dynamic_update_slice_in_dim(
+                both_d, local_next, (e_now + at) % kept_arr * v1, axis=0
+            )
     grads = lax.dot_general(
         row_slices, both_d, contract_rows, preferred_element_type=jnp.float32
     ).astype(jnp.bfloat16)

time: 240 us -> 265 us (1.10)
  the two profiles are of different devices: /device:TPU:1 before, /device:TPU:2 now
where the time goes in v1:
time: 265 us; the launch traced here: 264 us
  waiting for transfers between devices  124 us (47%)
  starting transfers between devices  49.4 us (19%)
  matrix products  28.1 us (11%)
  blocking collectives  26.5 us (10%)
  local copies, waits for them, and re-layouts  17.8 us (7%)
  between operations  14.2 us (5%)
  other arithmetic  4.16 us (2%)
    ppermute x8, waiting for transfers between devices, on_device(): lax.ppermute(current_value, 'dp', [(dev_i, (dev_i + 1) % kept_arr) for de...  56.6 us
    all_to_all x2, waiting for transfers between devices, gather_by_a2a(): lax.all_to_all(jnp.broadcast_to(x[None], (parts,) + x.shape), axis_name,...  31 us
    all_to_all x1, blocking collectives, gather_by_a2a(): lax.all_to_all(jnp.broadcast_to(x[None], (parts,) + x.shape), axis_name,...  26.5 us
    all_to_all x1, waiting for transfers between devices, on_device(): lax.all_to_all(row_blocks, 'dp', split_axis=0, concat_axis=0, tiled=True)  24.3 us
    ppermute x7, starting transfers between devices, on_device(): lax.ppermute(local_next, 'dp', [(dev_i, (dev_i - 1) % kept_arr) for dev_i...  20 us
    all_to_all x2, starting transfers between devices, gather_by_a2a(): lax.all_to_all(jnp.broadcast_to(x[None], (parts,) + x.shape), axis_name,...  15.6 us
    all_to_all x1, starting transfers between devices, on_device(): lax.all_to_all(picked_weight, 'dp', split_axis=0, concat_axis=0, tiled=True)  8.64 us
    dot_general x1, matrix products, on_device(): up = jnp.dot(row_x, full_w[1], preferred_element_type=jnp.float32)  5.87 us
  transfers between devices with their start and end apart: 21, of which 16 were waited for; matrix products, arithmetic and copies ran while one was open for 16% of the time, Pallas kernels for 0%

profile of v1, /device:TPU:2, one launch (start us, length us, event | category | flops | bytes accessed | tf_op | source)
XLA Modules:
  0.0 264.1 jit_solution(128910885240869428)
XLA Ops:
  7.2 1.9 pad_maximum_fusion.1
  9.2 0.7 all-gather.5.cloned.1.call-update
  9.9 1.0 copy.22
  10.9 1.5 broadcast_in_dim.8
  12.4 7.5 %all-to-all-start = ((bf16[16,256,256]{1,2,0:T(8,128)(2,1)}), bf16[16,256,256]{1,2,0:T(8,128)(2,1)}, u32[]{:S(2)}, u32[]{:S(2)}) async-start(bf16[16,256,256]{1,2,0:T(8,128)(2,1)} %broadcast_in_dim.8), calls=%async_computation | async-start | bytes 4194304 | tf_op jit(solution)/shard_map/all_to_all | solution.py:9
  19.9 0.8 fusion.22
  20.7 0.7 add_select_fusion.1
  21.5 25.7 %all-to-all-done = bf16[16,256,256]{1,2,0:T(8,128)(2,1)} async-done(((bf16[16,256,256]{1,2,0:T(8,128)(2,1)}), bf16[16,256,256]{1,2,0:T(8,128)(2,1)}, u32[]{:S(2)}, u32[]{:S(2)}) %all-to-all-start) | async-done | bytes 2097184 | tf_op jit(solution)/shard_map/all_to_all | solution.py:9
  47.2 4.2 %fusion.27 = f32[256,512]{1,0:T(8,128)S(1)} fusion(bf16[256,4096]{0,1:T(8,128)(2,1)} %bitcast.1, bf16[4096,512]{1,0:T(8,128)(2,1)} %param.10), kind=kOutput, calls=%fused_computation.59 | convolution fusion | flops 1073741824 | bytes 6815744 | tf_op jit(solution)/shard_map/dot_general | solution.py:54
  51.4 4.3 %fusion.14 = f32[256]{0:T(256)S(1)} fusion(bf16[256,4096]{0,1:T(8,128)(2,1)} %bitcast.1, bf16[4096,512]{1,0:T(8,128)(2,1)} %param.11, f32[256,512]{1,0:T(8,128)S(1)} %fusion.27, f32[512]{0:T(512)S(1)} %copy-done.2), kind=kOutput, calls=%fused_computation.16 | convolution fusion | flops 1074659072 | bytes 6818816 | tf_op jit(solution)/shard_map/dot_general | solution.py:55
  55.7 0.6 broadcast_in_dim.9
  56.3 8.1 %all-to-all-start.1 = ((f32[16,1,256]{2,1,0:T(1,128)}), f32[16,1,256]{2,1,0:T(1,128)S(1)}, u32[]{:S(2)}, u32[]{:S(2)}) async-start(f32[16,1,256]{2,1,0:T(1,128)} %broadcast_in_dim.9), calls=%async_computation.1 | async-start | bytes 32768 | tf_op jit(solution)/shard_map/all_to_all | solution.py:9
  64.4 0.7 constant_dynamic-slice_fusion.1
  65.1 0.1 eq.54
  65.2 0.1 and.98
  65.3 5.3 %all-to-all-done.1 = f32[16,1,256]{2,1,0:T(1,128)S(1)} async-done(((f32[16,1,256]{2,1,0:T(1,128)}), f32[16,1,256]{2,1,0:T(1,128)S(1)}, u32[]{:S(2)}, u32[]{:S(2)}) %all-to-all-start.1) | async-done | bytes 16416 | tf_op jit(solution)/shard_map/all_to_all | solution.py:9
  70.7 0.6 fusion.25
  71.3 2.5 fusion.6
  73.8 0.7 all_to_all.24
  74.5 8.6 %all-to-all-start.2 = ((bf16[16,1,192]{2,1,0:T(2,128)(2,1)}), bf16[16,1,192]{2,1,0:T(2,128)(2,1)S(1)}, u32[]{:S(2)}, u32[]{:S(2)}) async-start(bf16[16,1,192]{2,1,0:T(2,128)(2,1)} %all_to_all.24), calls=%async_computation.2 | async-start | bytes 32768 | tf_op jit(solution)/shard_map/all_to_all | solution.py:66
  83.2 2.4 fusion.15
  85.5 5.4 %all-to-all-done.2 = bf16[16,1,192]{2,1,0:T(2,128)(2,1)S(1)} async-done(((bf16[16,1,192]{2,1,0:T(2,128)(2,1)}), bf16[16,1,192]{2,1,0:T(2,128)(2,1)S(1)}, u32[]{:S(2)}, u32[]{:S(2)}) %all-to-all-start.2) | async-done | bytes 6176 | tf_op jit(solution)/shard_map/all_to_all | solution.py:66
  91.0 0.1 broadcast_in_dim.10
  91.1 26.5 %all_to_all.30 = bf16[16,192,256]{2,1,0:T(8,128)(2,1)} all-to-all(bf16[16,192,256]{2,1,0:T(8,128)(2,1)S(1)} %broadcast_in_dim.10), channel_id=1, replica_groups=mesh['dp'=16,'mp'=16] {'mp'}, dimensions={0} | all-to-all | bytes 3145728 | tf_op jit(solution)/shard_map/all_to_all | solution.py:9
  117.6 4.0 %all-to-all-start.4 = ((bf16[16,192,256]{2,1,0:T(8,128)(2,1)}), bf16[16,192,256]{2,1,0:T(8,128)(2,1)S(1)}, u32[]{:S(2)}, u32[]{:S(2)}) async-start(bf16[16,192,256]{2,1,0:T(8,128)(2,1)} %all_to_all.30), calls=%async_computation.4 | async-start | bytes 3145728 | tf_op jit(solution)/shard_map/all_to_all | solution.py:51
  121.7 1.6 copy.27
  123.3 5.8 %fusion = f32[192,896]{1,0:T(8,128)} fusion(bf16[192,4096]{1,0:T(8,128)(2,1)S(1)} %bitcast.20, bf16[4096,1152]{1,0:T(8,128)(2,1)} %all-gather.3.cloned.1.call-done), kind=kOutput, calls=%fused_computation | convolution fusion | flops 1409286144 | bytes 9601024 | tf_op jit(solution)/shard_map/dot_general | solution.py:68
  129.1 5.9 %multiply_convert_fusion = (bf16[192,896]{1,0:T(8,128)(2,1)}, bf16[192,896]{1,0:T(8,128)(2,1)S(1)}, bf16[192,896]{1,0:T(8,128)(2,1)S(1)}) fusion(f32[192,896]{1,0:T(8,128)} %fusion, f32[192]{0:T(256)S(1)} %convert_reduce_fusion, bf16[192,896]{1,0:T(8,128)(2,1)S(1)} %copy-done.1, bf16[192,4096]{1,0:T(8,128)(2,1)S(1)} %bitcast.21, ...), kind=kOutput, calls=%fused_computation.19 | convolution fusion | flops 1412382720 | bytes 10978048 | tf_op jit(solution)/shard_map/dot_general | solution.py:69
  135.0 0.1 pad_maximum_fusion
  135.0 24.3 %all-to-all-done.4 = bf16[16,192,256]{2,1,0:T(8,128)(2,1)S(1)} async-done(((bf16[16,192,256]{2,1,0:T(8,128)(2,1)}), bf16[16,192,256]{2,1,0:T(8,128)(2,1)S(1)}, u32[]{:S(2)}, u32[]{:S(2)}) %all-to-all-start.4) | async-done | bytes 1572896 | tf_op jit(solution)/shard_map/all_to_all | solution.py:51
  159.3 1.1 collective-permute-start
  160.4 1.9 collective-permute-start.1
  162.3 8.7 %collective-permute-done = bf16[192,1792]{1,0:T(8,128)(2,1)} collective-permute-done((bf16[192,1792]{1,0:T(8,128)(2,1)S(1)}, bf16[192,1792]{1,0:T(8,128)(2,1)}, u32[]{:S(2)}, u32[]{:S(2)}) %collective-permute-start) | collective-permute-done | bytes 688160 | tf_op jit(solution)/shard_map/ppermute | solution.py:86
  171.0 3.0 %collective-permute-start.3 = (bf16[192,1792]{1,0:T(8,128)(2,1)}, bf16[192,1792]{1,0:T(8,128)(2,1)}, u32[]{:S(2)}, u32[]{:S(2)}) collective-permute-start(bf16[192,1792]{1,0:T(8,128)(2,1)} %collective-permute-done.1), channel_id=1, source_target_pairs={{0,240},{16,0},{32,16},{48,32},{64,48},{80,64},{96,80},{112,96},{1... | collective-permute-start | bytes 2064392 | tf_op jit(solution)/shard_map/ppermute | solution.py:93
  174.0 8.9 %collective-permute-done.2 = bf16[192,1792]{1,0:T(8,128)(2,1)} collective-permute-done((bf16[192,1792]{1,0:T(8,128)(2,1)}, bf16[192,1792]{1,0:T(8,128)(2,1)}, u32[]{:S(2)}, u32[]{:S(2)}) %collective-permute-start.2) | collective-permute-done | bytes 688160 | tf_op jit(solution)/shard_map/ppermute | solution.py:86
  182.9 3.0 %collective-permute-start.5 = (bf16[192,1792]{1,0:T(8,128)(2,1)}, bf16[192,1792]{1,0:T(8,128)(2,1)}, u32[]{:S(2)}, u32[]{:S(2)}) collective-permute-start(bf16[192,1792]{1,0:T(8,128)(2,1)} %collective-permute-done.3), channel_id=1, source_target_pairs={{0,240},{16,0},{32,16},{48,32},{64,48},{80,64},{96,80},{112,96},{1... | collective-permute-start | bytes 2064392 | tf_op jit(solution)/shard_map/ppermute | solution.py:93
  185.8 8.9 %collective-permute-done.4 = bf16[192,1792]{1,0:T(8,128)(2,1)} collective-permute-done((bf16[192,1792]{1,0:T(8,128)(2,1)}, bf16[192,1792]{1,0:T(8,128)(2,1)}, u32[]{:S(2)}, u32[]{:S(2)}) %collective-permute-start.4) | collective-permute-done | bytes 688160 | tf_op jit(solution)/shard_map/ppermute | solution.py:86
  194.8 0.7 broadcast_in_dim.11
  195.5 1.2 constant_dynamic-update-slice_fusion.15
  196.7 1.2 constant_dynamic-update-slice_fusion.14
  197.8 3.0 %collective-permute-start.7 = (bf16[192,1792]{1,0:T(8,128)(2,1)}, bf16[192,1792]{1,0:T(8,128)(2,1)S(1)}, u32[]{:S(2)}, u32[]{:S(2)}) collective-permute-start(bf16[192,1792]{1,0:T(8,128)(2,1)} %collective-permute-done.5), channel_id=1, source_target_pairs={{0,240},{16,0},{32,16},{48,32},{64,48},{80,64},{96,80},{112,96},{1... | collective-permute-start | bytes 2064392 | tf_op jit(solution)/shard_map/ppermute | solution.py:93
  200.8 1.1 constant_dynamic-update-slice_fusion.13
  201.9 4.7 %collective-permute-done.6 = bf16[192,1792]{1,0:T(8,128)(2,1)} collective-permute-done((bf16[192,1792]{1,0:T(8,128)(2,1)}, bf16[192,1792]{1,0:T(8,128)(2,1)}, u32[]{:S(2)}, u32[]{:S(2)}) %collective-permute-start.6) | collective-permute-done | bytes 688160 | tf_op jit(solution)/shard_map/ppermute | solution.py:86
  206.7 1.1 constant_dynamic-update-slice_fusion.12
  207.8 1.2 constant_dynamic-update-slice_fusion.11
  209.0 0.6 collective-permute-done.7
  209.6 3.0 %collective-permute-start.9 = (bf16[192,1792]{1,0:T(8,128)(2,1)S(1)}, bf16[192,1792]{1,0:T(8,128)(2,1)S(1)}, u32[]{:S(2)}, u32[]{:S(2)}) collective-permute-start(bf16[192,1792]{1,0:T(8,128)(2,1)S(1)} %collective-permute-done.7), channel_id=1, source_target_pairs={{0,240},{16,0},{32,16},{48,32},{64,48},{80,64},{96,80},{112,96},{1... | collective-permute-start | bytes 2064392 | tf_op jit(solution)/shard_map/ppermute | solution.py:93
  212.6 1.1 constant_dynamic-update-slice_fusion.10
  213.7 4.7 %collective-permute-done.8 = bf16[192,1792]{1,0:T(8,128)(2,1)S(1)} collective-permute-done((bf16[192,1792]{1,0:T(8,128)(2,1)}, bf16[192,1792]{1,0:T(8,128)(2,1)S(1)}, u32[]{:S(2)}, u32[]{:S(2)}) %collective-permute-start.8) | collective-permute-done | bytes 688160 | tf_op jit(solution)/shard_map/ppermute | solution.py:86
  218.4 1.1 constant_dynamic-update-slice_fusion.9
  219.6 1.2 constant_dynamic-update-slice_fusion.8
  220.8 0.3 collective-permute-done.9
  221.0 3.1 %collective-permute-start.11 = (bf16[192,1792]{1,0:T(8,128)(2,1)S(1)}, bf16[192,1792]{1,0:T(8,128)(2,1)S(1)}, u32[]{:S(2)}, u32[]{:S(2)}) collective-permute-start(bf16[192,1792]{1,0:T(8,128)(2,1)S(1)} %collective-permute-done.9), channel_id=1, source_target_pairs={{0,240},{16,0},{32,16},{48,32},{64,48},{80,64},{96,80},{112,96},{1... | collective-permute-start | bytes 2064392 | tf_op jit(solution)/shard_map/ppermute | solution.py:93
  224.1 0.1 constant_dynamic-update-slice_fusion.7
  224.2 5.8 %collective-permute-done.10 = bf16[192,1792]{1,0:T(8,128)(2,1)S(1)} collective-permute-done((bf16[192,1792]{1,0:T(8,128)(2,1)S(1)}, bf16[192,1792]{1,0:T(8,128)(2,1)S(1)}, u32[]{:S(2)}, u32[]{:S(2)}) %collective-permute-start.10) | collective-permute-done | bytes 688160 | tf_op jit(solution)/shard_map/ppermute | solution.py:86
  230.1 0.1 constant_dynamic-update-slice_fusion.5
  230.1 2.5 collective-permute-done.11
  232.6 3.1 %collective-permute-start.13 = (bf16[192,1792]{1,0:T(8,128)(2,1)S(1)}, bf16[192,1792]{1,0:T(8,128)(2,1)S(1)}, u32[]{:S(2)}, u32[]{:S(2)}) collective-permute-start(bf16[192,1792]{1,0:T(8,128)(2,1)S(1)} %collective-permute-done.11), channel_id=1, source_target_pairs={{0,240},{16,0},{32,16},{48,32},{64,48},{80,64},{96,80},{112,96},{1... | collective-permute-start | bytes 2064392 | tf_op jit(solution)/shard_map/ppermute | solution.py:93
  235.8 5.8 %collective-permute-done.12 = bf16[192,1792]{1,0:T(8,128)(2,1)S(1)} collective-permute-done((bf16[192,1792]{1,0:T(8,128)(2,1)S(1)}, bf16[192,1792]{1,0:T(8,128)(2,1)S(1)}, u32[]{:S(2)}, u32[]{:S(2)}) %collective-permute-start.12) | collective-permute-done | bytes 688160 | tf_op jit(solution)/shard_map/ppermute | solution.py:86
  241.7 0.1 constant_dynamic-update-slice_fusion.2
  241.7 2.5 collective-permute-done.13
  244.2 8.9 %collective-permute-done.14 = bf16[192,1792]{1,0:T(8,128)(2,1)S(1)} collective-permute-done((bf16[192,1792]{1,0:T(8,128)(2,1)S(1)}, bf16[192,1792]{1,0:T(8,128)(2,1)S(1)}, u32[]{:S(2)}, u32[]{:S(2)}) %collective-permute-start.14) | collective-permute-done | bytes 688160 | tf_op jit(solution)/shard_map/ppermute | solution.py:86
  253.2 3.0 %convolution_convert_fusion = bf16[256,1792]{1,0:T(8,128)(2,1)S(1)} fusion(bf16[3072,256]{1,0:T(8,128)(2,1)S(1)} %bitcast.19, bf16[3072,1792]{1,0:T(8,128)(2,1)S(1)} %constant_dynamic-update-slice_fusion), kind=kOutput, calls=%fused_computation.8 | convolution fusion | flops 2819031040 | bytes 13500416 | tf_op jit(solution)/shard_map/dot_general | solution.py:99
  256.3 1.0 fusion.26
  (31 shorter events, 0.5 us)
Async XLA Ops:
  7.2 44.2 %copy-start.2 = (f32[512]{0:T(512)S(1)}, f32[512]{0:T(512)}, u32[]{:S(2)}) copy-start(f32[512]{0:T(512)} %param.12) | copy-start | bytes 6148
  7.2 76.0 %all-gather.3.cloned.1.call-start = ((), (), s32[]{:S(2)}) async-start(), calls=%async_computation.5 | async-start | bytes 10027008 | tf_op jit(solution)/shard_map/all_gather | solution.py:28
  9.2 119.9 %all-gather.5.cloned.1.call-start = ((), (), s32[]{:S(2)}) async-start(), calls=%async_computation.6 | async-start | bytes 7798784 | tf_op jit(solution)/shard_map/all_gather | solution.py:30
  12.4 34.7 %all-to-all-start = ((bf16[16,256,256]{1,2,0:T(8,128)(2,1)}), bf16[16,256,256]{1,2,0:T(8,128)(2,1)}, u32[]{:S(2)}, u32[]{:S(2)}) async-start(bf16[16,256,256]{1,2,0:T(8,128)(2,1)} %broadcast_in_dim.8), calls=%async_computation | async-start | bytes 4194304 | tf_op jit(solution)/shard_map/all_to_all | solution.py:9
  56.3 14.3 %all-to-all-start.1 = ((f32[16,1,256]{2,1,0:T(1,128)}), f32[16,1,256]{2,1,0:T(1,128)S(1)}, u32[]{:S(2)}, u32[]{:S(2)}) async-start(f32[16,1,256]{2,1,0:T(1,128)} %broadcast_in_dim.9), calls=%async_computation.1 | async-start | bytes 32768 | tf_op jit(solution)/shard_map/all_to_all | solution.py:9
  74.5 16.5 %all-to-all-start.2 = ((bf16[16,1,192]{2,1,0:T(2,128)(2,1)}), bf16[16,1,192]{2,1,0:T(2,128)(2,1)S(1)}, u32[]{:S(2)}, u32[]{:S(2)}) async-start(bf16[16,1,192]{2,1,0:T(2,128)(2,1)} %all_to_all.24), calls=%async_computation.2 | async-start | bytes 32768 | tf_op jit(solution)/shard_map/all_to_all | solution.py:66
  117.6 11.5 %copy-start.1 = (bf16[192,896]{1,0:T(8,128)(2,1)S(1)}, bf16[192,896]{1,0:T(8,128)(2,1)}, u32[]{:S(2)}) copy-start(bf16[192,896]{1,0:T(8,128)(2,1)} %param.17) | copy-start | bytes 1032196
  117.6 41.7 %all-to-all-start.4 = ((bf16[16,192,256]{2,1,0:T(8,128)(2,1)}), bf16[16,192,256]{2,1,0:T(8,128)(2,1)S(1)}, u32[]{:S(2)}, u32[]{:S(2)}) async-start(bf16[16,192,256]{2,1,0:T(8,128)(2,1)} %all_to_all.30), calls=%async_computation.4 | async-start | bytes 3145728 | tf_op jit(solution)/shard_map/all_to_all | solution.py:51
  135.0 59.7 %copy-start = (bf16[192,1792]{1,0:T(8,128)(2,1)}, bf16[192,1792]{1,0:T(8,128)(2,1)S(1)}, u32[]{:S(2)}) copy-start(bf16[192,1792]{1,0:T(8,128)(2,1)S(1)} %pad_maximum_fusion) | copy-start | bytes 2064388
  159.3 11.7 %collective-permute-start = (bf16[192,1792]{1,0:T(8,128)(2,1)S(1)}, bf16[192,1792]{1,0:T(8,128)(2,1)}, u32[]{:S(2)}, u32[]{:S(2)}) collective-permute-start(bf16[192,1792]{1,0:T(8,128)(2,1)S(1)} %pad_maximum_fusion), channel_id=1, source_target_pairs={{0,16},{16,32},{32,48},{48,64},{64,80},{80,96},{96,112},{112,128},... | collective-permute-start | bytes 2064392 | tf_op jit(solution)/shard_map/ppermute | solution.py:86
  160.4 10.6 %collective-permute-start.1 = (bf16[192,1792]{1,0:T(8,128)(2,1)S(1)}, bf16[192,1792]{1,0:T(8,128)(2,1)}, u32[]{:S(2)}, u32[]{:S(2)}) collective-permute-start(bf16[192,1792]{1,0:T(8,128)(2,1)S(1)} %pad_maximum_fusion), channel_id=1, source_target_pairs={{0,240},{16,0},{32,16},{48,32},{64,48},{80,64},{96,80},{112,96},{1... | collective-permute-start | bytes 2064392 | tf_op jit(solution)/shard_map/ppermute | solution.py:93
  171.0 11.9 %collective-permute-start.2 = (bf16[192,1792]{1,0:T(8,128)(2,1)}, bf16[192,1792]{1,0:T(8,128)(2,1)}, u32[]{:S(2)}, u32[]{:S(2)}) collective-permute-start(bf16[192,1792]{1,0:T(8,128)(2,1)} %collective-permute-done), channel_id=1, source_target_pairs={{0,16},{16,32},{32,48},{48,64},{64,80},{80,96},{96,112},{112,128},... | collective-permute-start | bytes 2064392 | tf_op jit(solution)/shard_map/ppermute | solution.py:86
  171.0 11.9 %collective-permute-start.3 = (bf16[192,1792]{1,0:T(8,128)(2,1)}, bf16[192,1792]{1,0:T(8,128)(2,1)}, u32[]{:S(2)}, u32[]{:S(2)}) collective-permute-start(bf16[192,1792]{1,0:T(8,128)(2,1)} %collective-permute-done.1), channel_id=1, source_target_pairs={{0,240},{16,0},{32,16},{48,32},{64,48},{80,64},{96,80},{112,96},{1... | collective-permute-start | bytes 2064392 | tf_op jit(solution)/shard_map/ppermute | solution.py:93
  182.9 11.9 %collective-permute-start.4 = (bf16[192,1792]{1,0:T(8,128)(2,1)}, bf16[192,1792]{1,0:T(8,128)(2,1)}, u32[]{:S(2)}, u32[]{:S(2)}) collective-permute-start(bf16[192,1792]{1,0:T(8,128)(2,1)} %collective-permute-done.2), channel_id=1, source_target_pairs={{0,16},{16,32},{32,48},{48,64},{64,80},{80,96},{96,112},{112,128},... | collective-permute-start | bytes 2064392 | tf_op jit(solution)/shard_map/ppermute | solution.py:86
  182.9 14.9 %collective-permute-start.5 = (bf16[192,1792]{1,0:T(8,128)(2,1)}, bf16[192,1792]{1,0:T(8,128)(2,1)}, u32[]{:S(2)}, u32[]{:S(2)}) collective-permute-start(bf16[192,1792]{1,0:T(8,128)(2,1)} %collective-permute-done.3), channel_id=1, source_target_pairs={{0,240},{16,0},{32,16},{48,32},{64,48},{80,64},{96,80},{112,96},{1... | collective-permute-start | bytes 2064392 | tf_op jit(solution)/shard_map/ppermute | solution.py:93
  194.8 11.9 %collective-permute-start.6 = (bf16[192,1792]{1,0:T(8,128)(2,1)}, bf16[192,1792]{1,0:T(8,128)(2,1)}, u32[]{:S(2)}, u32[]{:S(2)}) collective-permute-start(bf16[192,1792]{1,0:T(8,128)(2,1)} %collective-permute-done.4), channel_id=1, source_target_pairs={{0,16},{16,32},{32,48},{48,64},{64,80},{80,96},{96,112},{112,128},... | collective-permute-start | bytes 2064392 | tf_op jit(solution)/shard_map/ppermute | solution.py:86
  197.8 11.7 %collective-permute-start.7 = (bf16[192,1792]{1,0:T(8,128)(2,1)}, bf16[192,1792]{1,0:T(8,128)(2,1)S(1)}, u32[]{:S(2)}, u32[]{:S(2)}) collective-permute-start(bf16[192,1792]{1,0:T(8,128)(2,1)} %collective-permute-done.5), channel_id=1, source_target_pairs={{0,240},{16,0},{32,16},{48,32},{64,48},{80,64},{96,80},{112,96},{1... | collective-permute-start | bytes 2064392 | tf_op jit(solution)/shard_map/ppermute | solution.py:93
  206.7 11.8 %collective-permute-start.8 = (bf16[192,1792]{1,0:T(8,128)(2,1)}, bf16[192,1792]{1,0:T(8,128)(2,1)S(1)}, u32[]{:S(2)}, u32[]{:S(2)}) collective-permute-start(bf16[192,1792]{1,0:T(8,128)(2,1)} %collective-permute-done.6), channel_id=1, source_target_pairs={{0,16},{16,32},{32,48},{48,64},{64,80},{80,96},{96,112},{112,128},... | collective-permute-start | bytes 2064392 | tf_op jit(solution)/shard_map/ppermute | solution.py:86
  209.6 11.5 %collective-permute-start.9 = (bf16[192,1792]{1,0:T(8,128)(2,1)S(1)}, bf16[192,1792]{1,0:T(8,128)(2,1)S(1)}, u32[]{:S(2)}, u32[]{:S(2)}) collective-permute-start(bf16[192,1792]{1,0:T(8,128)(2,1)S(1)} %collective-permute-done.7), channel_id=1, source_target_pairs={{0,240},{16,0},{32,16},{48,32},{64,48},{80,64},{96,80},{112,96},{1... | collective-permute-start | bytes 2064392 | tf_op jit(solution)/shard_map/ppermute | solution.py:93
  218.4 11.6 %collective-permute-start.10 = (bf16[192,1792]{1,0:T(8,128)(2,1)S(1)}, bf16[192,1792]{1,0:T(8,128)(2,1)S(1)}, u32[]{:S(2)}, u32[]{:S(2)}) collective-permute-start(bf16[192,1792]{1,0:T(8,128)(2,1)S(1)} %collective-permute-done.8), channel_id=1, source_target_pairs={{0,16},{16,32},{32,48},{48,64},{64,80},{80,96},{96,112},{112,128},... | collective-permute-start | bytes 2064392 | tf_op jit(solution)/shard_map/ppermute | solution.py:86
  221.0 11.6 %collective-permute-start.11 = (bf16[192,1792]{1,0:T(8,128)(2,1)S(1)}, bf16[192,1792]{1,0:T(8,128)(2,1)S(1)}, u32[]{:S(2)}, u32[]{:S(2)}) collective-permute-start(bf16[192,1792]{1,0:T(8,128)(2,1)S(1)} %collective-permute-done.9), channel_id=1, source_target_pairs={{0,240},{16,0},{32,16},{48,32},{64,48},{80,64},{96,80},{112,96},{1... | collective-permute-start | bytes 2064392 | tf_op jit(solution)/shard_map/ppermute | solution.py:93
  230.0 11.6 %collective-permute-start.12 = (bf16[192,1792]{1,0:T(8,128)(2,1)S(1)}, bf16[192,1792]{1,0:T(8,128)(2,1)S(1)}, u32[]{:S(2)}, u32[]{:S(2)}) collective-permute-start(bf16[192,1792]{1,0:T(8,128)(2,1)S(1)} %collective-permute-done.10), channel_id=1, source_target_pairs={{0,16},{16,32},{32,48},{48,64},{64,80},{80,96},{96,112},{112,128},... | collective-permute-start | bytes 2064392 | tf_op jit(solution)/shard_map/ppermute | solution.py:86
  232.6 11.6 %collective-permute-start.13 = (bf16[192,1792]{1,0:T(8,128)(2,1)S(1)}, bf16[192,1792]{1,0:T(8,128)(2,1)S(1)}, u32[]{:S(2)}, u32[]{:S(2)}) collective-permute-start(bf16[192,1792]{1,0:T(8,128)(2,1)S(1)} %collective-permute-done.11), channel_id=1, source_target_pairs={{0,240},{16,0},{32,16},{48,32},{64,48},{80,64},{96,80},{112,96},{1... | collective-permute-start | bytes 2064392 | tf_op jit(solution)/shard_map/ppermute | solution.py:93
  241.6 11.6 %collective-permute-start.14 = (bf16[192,1792]{1,0:T(8,128)(2,1)S(1)}, bf16[192,1792]{1,0:T(8,128)(2,1)S(1)}, u32[]{:S(2)}, u32[]{:S(2)}) collective-permute-start(bf16[192,1792]{1,0:T(8,128)(2,1)S(1)} %collective-permute-done.12), channel_id=1, source_target_pairs={{0,16},{16,32},{32,48},{48,64},{64,80},{80,96},{96,112},{112,128},... | collective-permute-start | bytes 2064392 | tf_op jit(solution)/shard_map/ppermute | solution.py:86
Sparse Core Ops, SparseCore 0:
  9.8 63.7 all-gather.2
  75.4 49.6 all-gather.4
